TPU v7x, 32 devices: a whole 2x2x4 slice. The times are simulated.
32 devices in a mesh: depth: 4 (over z), row: 2 (over core), col: 4 (over y, x).
Axes of the slice: x: 2, y: 2, z: 4, core: 2. Of those that a mesh axis runs over, the one named last changes fastest.
Arguments:
- volume: bfloat16 [4, 18, 256, 8192], P('depth', None, 'row', 'col'), may hold values from -6 to 6
- order: int32 [4], replicated, may hold values from 0 to 3, each once
- empty: int32 [4, 2, 4], P('depth', 'row', 'col'), may hold values 0 or 1
- bump_center: float32 [4], replicated, may hold values from -1.5 to 1.5
- bump_width: float32 [4], replicated, may hold values from 0.3 to 1
- bump_height: float32 [4], replicated, may hold values from 0.5 to 4
- bump_color: float32 [3, 4], replicated, may hold values from 0.5 to 2
- light_dir: float32 [3], replicated, may hold values from -1 to 1
Outputs:
- image: float32 [2, 4, 128, 8192], P('row', None, 'depth', 'col')
Inputs may be any that keep to these rules, and one draw needn't show every extreme that they name: `order`: a permutation of the depth indices.
All inputs are finite; a program needn't handle non-finite values. No bound on the sum of `empty` on one device may be relied on, other than what follows from the above.
Results may differ from a plain program's by a relative error of at most 0.0003.
Values may be sent and summed in bfloat16 or wider, within the bound.
No kernel may reach another device: no remote copies, remote signals or barrier semaphores. Data moves between devices by JAX's collectives and lax.ppermute only.
A program may use at most 128 MiB of HBM per device.

v0:
```python
import jax
import jax.numpy as jnp
from jax import lax
from jax.sharding import PartitionSpec as P

slab_depth = 8
absorption = 0.08


def with_halo(x, sides, width):
    for axis, dim in sides:
        count, length = (lax.axis_size(axis), x.shape[dim])
        up = [(i, (i + 1) % count) for i in range(count - 1)]
        down = [(j, i) for i, j in up]
        last = lax.slice_in_dim(x, length - width, length, axis=dim)
        leading = lax.slice_in_dim(x, 0, width, axis=dim)
        before = lax.ppermute(last, axis, up)
        after = lax.ppermute(leading, axis, down)
        x = jnp.concatenate([before, x, after], axis=dim)
    return x


def march_brick(padded, bump_center, bump_width, bump_height, bump_color, light_dir):
    depth_len = padded.shape[0] - 2
    row_count = padded.shape[1] - 2
    col_count = padded.shape[2] - 2
    per_sample = absorption / depth_len

    def advance(state_pair, slab_index):
        through, radiance = state_pair
        block_cells = lax.dynamic_slice_in_dim(
            padded, slab_index * slab_depth, slab_depth + 2, 0
        ).astype(jnp.float32)
        samples = block_cells[1:-1, 1:-1, 1:-1]
        grad_z = 0.5 * (block_cells[2:, 1:-1, 1:-1] - block_cells[:-2, 1:-1, 1:-1])
        grad_y = 0.5 * (block_cells[1:-1, 2:, 1:-1] - block_cells[1:-1, :-2, 1:-1])
        grad_x = 0.5 * (block_cells[1:-1, 1:-1, 2:] - block_cells[1:-1, 1:-1, :-2])
        facing = jnp.abs(light_dir[0] * grad_z + light_dir[1] * grad_y + light_dir[2] * grad_x)
        shading = 0.3 + 0.7 * facing / jnp.sqrt(
            grad_z * grad_z + grad_y * grad_y + grad_x * grad_x + 1.0
        )
        density = jnp.zeros_like(samples)
        emission = [jnp.zeros_like(samples) for channel in range(3)]
        for bump_index in range(bump_center.shape[0]):
            offset = samples - bump_center[bump_index]
            bump_value = jnp.exp(
                -offset * offset / (2.0 * bump_width[bump_index] * bump_width[bump_index])
            )
            density = density + bump_height[bump_index] * bump_value
            emission = [
                emission[channel] + bump_color[channel, bump_index] * bump_value
                for channel in range(3)
            ]
        passing = jnp.exp(-per_sample * density)
        inclusive = jnp.cumprod(passing, axis=0)
        transmit = jnp.concatenate([jnp.ones_like(passing[:1]), inclusive[:-1]], 0) * through
        weights = transmit * (1.0 - passing) * shading
        radiance = radiance + jnp.stack(
            [jnp.sum(weights * emission[channel], 0) for channel in range(3)]
        )
        return ((through * inclusive[-1], radiance), None)

    start_carry = (
        jnp.ones((row_count, col_count), jnp.float32),
        jnp.zeros((3, row_count, col_count), jnp.float32),
    )
    (through, radiance), unused = lax.scan(
        advance, start_carry, jnp.arange(depth_len // slab_depth, dtype=jnp.int32)
    )
    return jnp.concatenate([radiance, (1.0 - through)[None]], 0)


def composite(stacked, order):
    ranked = jnp.take(stacked, order, axis=0)

    def layer_over(state_pair, layer_image):
        through, summed = state_pair
        summed = summed + through[None] * layer_image
        return ((through * (1.0 - layer_image[3]), summed), None)

    start_carry = (
        jnp.ones(stacked.shape[2:], jnp.float32),
        jnp.zeros(stacked.shape[1:], jnp.float32),
    )
    (through, summed), unused = lax.scan(layer_over, start_carry, ranked)
    return summed


def per_device(volume, order, empty, bump_center, bump_width, bump_height, bump_color, light_dir):
    padded = with_halo(volume[0], (("row", 1), ("col", 2)), 1)
    row_count = volume.shape[2]
    col_count = volume.shape[3]

    def blank_layer():
        return jnp.zeros((4, row_count, col_count), jnp.float32)

    def lit_layer():
        return march_brick(padded, bump_center, bump_width, bump_height, bump_color, light_dir)

    layer_image = lax.cond(empty[0, 0, 0] == 1, blank_layer, lit_layer)
    band_rows = composite(
        lax.all_to_all(layer_image[None], "depth", split_axis=2, concat_axis=0, tiled=True), order
    )
    return band_rows[None]


def solution(mesh):
    placed = (
        P("depth", None, "row", "col"),
        P(),
        P("depth", "row", "col"),
        P(),
        P(),
        P(),
        P(),
        P(),
    )
    return jax.shard_map(
        per_device,
        mesh=mesh,
        in_specs=placed,
        out_specs=P("row", None, "depth", "col"),
        check_vma=False,
    )
```

profile of v0, /device:TPU:5, one launch (start us, length us, event | category | flops | bytes accessed | tf_op | source)
XLA Modules:
  0.0 430.9 jit_solution(2655064788858189192)
XLA Ops:
  0.0 11.8 %copy.50 = bf16[1,18,128,2048]{3,1,2,0:T(8,128)(2,1)S(1)} copy(bf16[1,18,128,2048]{3,2,1,0:T(8,128)(2,1)} %param.14) | data formatting | bytes 18874368 | tf_op args[0]
  11.8 1.3 collective-permute-start
  13.1 3.0 collective-permute-start.1
  17.1 3.0 pad_maximum_fusion.1
  20.1 4.6 %copy-done.2 = bf16[18,130,2048]{2,0,1:T(8,128)(2,1)} copy-done((bf16[18,130,2048]{2,0,1:T(8,128)(2,1)}, bf16[18,130,2048]{2,0,1:T(8,128)(2,1)S(1)}, u32[]{:S(2)}) %copy-start.2) | copy-done | bytes 9584664
  25.7 3.1 collective-permute-start.2
  29.5 3.1 collective-permute-start.3
  33.3 11.0 %copy.40 = bf16[18,130,2048]{2,1,0:T(8,128)(2,1)} copy(bf16[18,130,2048]{2,0,1:T(8,128)(2,1)} %copy-done.2) | data formatting | bytes 19169280 | tf_op jit(solution)/shard_map/concatenate | solution.py:19
  45.1 19.2 %concatenate.13 = bf16[18,130,2050]{2,1,0:T(8,128)(2,1)} concatenate(bf16[18,130,1]{2,1,0:T(8,128)(2,1)S(1)} %copy.39, bf16[18,130,2048]{2,1,0:T(8,128)(2,1)} %copy.40, bf16[18,130,1]{2,1,0:T(8,128)(2,1)S(1)} %copy.41), dimensions={2} | concatenate | bytes 19188000 | tf_op jit(solution)/shard_map/concatenate | solution.py:19
  64.3 2.5 conditional.1
  64.3 2.5 broadcast.64
  66.8 6.9 %copy.52 = f32[4,128,2048]{2,0,1:T(4,128)} copy(f32[4,128,2048]{2,1,0:T(8,128)} %get-tuple-element.623) | data formatting | bytes 8388608 | tf_op jit(solution)/shard_map/cond | solution.py:100
  73.6 234.6 %all-to-all-start = ((f32[1,4,128,2048]{3,1,0,2:T(4,128)}), f32[1,4,128,2048]{3,1,0,2:T(4,128)}, u32[]{:S(2)}, u32[]{:S(2)}) async-start(f32[1,4,128,2048]{3,1,0,2:T(4,128)} %bitcast.118), calls=%async_computation | async-start | bytes 8388608 | tf_op jit(solution)/shard_map/all_to_all | solution.py:102
  308.3 94.6 %all-to-all-done = f32[1,4,128,2048]{3,1,0,2:T(4,128)} async-done(((f32[1,4,128,2048]{3,1,0,2:T(4,128)}), f32[1,4,128,2048]{3,1,0,2:T(4,128)}, u32[]{:S(2)}, u32[]{:S(2)}) %all-to-all-start) | async-done | bytes 4194336 | tf_op jit(solution)/shard_map/all_to_all | solution.py:102
  402.9 6.6 %copy.51 = f32[1,4,4,32,2048]{4,3,1,2,0:T(8,128)} copy(f32[1,4,4,32,2048]{4,1,3,2,0:T(4,128)} %bitcast.11) | data formatting | bytes 8388608 | tf_op jit(solution)/shard_map/all_to_all | solution.py:102
  409.5 5.0 %gather_fusion = f32[4,4,32,2048]{3,2,1,0:T(8,128)} fusion(f32[4,4,32,2048]{3,2,1,0:T(8,128)} %bitcast.119, s32[1024]{0:T(1024)S(1)} %pad_clamp_fusion), kind=kCustom, calls=%fused_computation | custom fusion | bytes 8388624 | tf_op jit(solution)/shard_map/jit(_take)/gather | solution.py:74
  414.4 4.9 %broadcast_select_fusion.2 = f32[4,4,32,2048]{3,2,1,0:T(8,128)} fusion(f32[4,4,32,2048]{3,2,1,0:T(8,128)} %gather_fusion, pred[4]{0:T(512)(128)(4,1)S(1)} %compare_and_fusion), kind=kLoop, calls=%fused_computation.39 | loop fusion | flops 1048576 | bytes 8388612 | tf_op jit(solution)/shard_map/jit(_take)/select_n | solution.py:74
  419.3 10.6 %while.28 = (s32[]{:T(128)}, f32[32,2048]{1,0:T(8,128)S(1)}, f32[4,32,2048]{2,1,0:T(8,128)S(1)}, f32[4,4,32,2048]{3,2,1,0:T(8,128)}, s32[]{:T(128)}, /*index=5*/s32[]{:T(128)}, s32[]{}) while((s32[]{:T(128)}, f32[32,2048]{1,0:T(8,128)S(1)}, f32[4,32,2048]{2,1,0:T(8,128)S(1)}, f32[4,4,32,2048]{3,2,1,0:T(8,128)}, s32[]{:T(128)}, ...), condition=%wide.region_9.10_spmd.clone, body=%wide.region_8.9_spmd.clone.sunk | while | flops 983044 | bytes 4456560 | solution.py:85
  420.3 1.6 fusion.27
  422.0 1.0 fusion.26
  423.0 1.6 fusion.27
  424.6 1.0 fusion.26
  425.7 1.6 fusion.27
  428.3 1.6 fusion.27
  (26 shorter events, 6.5 us)
Async XLA Ops:
  11.8 4.3 %collective-permute-start = (bf16[18,1,2048]{2,0,1:T(8,128)(2,1)S(1)}, bf16[18,1,2048]{2,0,1:T(8,128)(2,1)S(1)}, u32[]{:S(2)}, u32[]{:S(2)}) collective-permute-start(bf16[18,1,2048]{2,0,1:T(8,128)(2,1)S(1)} %get-tuple-element.371), channel_id=1, source_target_pairs={{0,4},{1,5},{2,6},{3,7},{8,12},{9,13},{10,14},{11,15},{16,20},{17,... | collective-permute-start | bytes 221192 | tf_op jit(solution)/shard_map/ppermute | solution.py:17
  13.1 4.0 collective-permute-start.1
  20.0 4.6 %copy-start.2 = (bf16[18,130,2048]{2,0,1:T(8,128)(2,1)}, bf16[18,130,2048]{2,0,1:T(8,128)(2,1)S(1)}, u32[]{:S(2)}) copy-start(bf16[18,130,2048]{2,0,1:T(8,128)(2,1)S(1)} %pad_maximum_fusion.1) | copy-start | bytes 28753924
  25.7 18.5 %collective-permute-start.2 = (bf16[18,130,1]{1,0,2:T(8,128)(2,1)S(1)}, bf16[18,130,1]{1,0,2:T(8,128)(2,1)S(1)}, u32[]{:S(2)}, u32[]{:S(2)}) collective-permute-start(bf16[18,130,1]{1,0,2:T(8,128)(2,1)S(1)} %copy.37), channel_id=1, source_target_pairs={{0,1},{1,2},{2,3},{4,5},{5,6},{6,7},{8,9},{9,10},{10,11},{12,13},{... | collective-permute-start | bytes 14048 | tf_op jit(solution)/shard_map/ppermute | solution.py:17
  29.5 15.1 %collective-permute-start.3 = (bf16[18,130,1]{1,0,2:T(8,128)(2,1)S(1)}, bf16[18,130,1]{1,0,2:T(8,128)(2,1)S(1)}, u32[]{:S(2)}, u32[]{:S(2)}) collective-permute-start(bf16[18,130,1]{1,0,2:T(8,128)(2,1)S(1)} %copy.38), channel_id=1, source_target_pairs={{1,0},{2,1},{3,2},{5,4},{6,5},{7,6},{9,8},{10,9},{11,10},{13,12},{... | collective-permute-start | bytes 14048 | tf_op jit(solution)/shard_map/ppermute | solution.py:18
  45.0 19.3 %copy-start.7 = (f32[4]{0:T(128)S(1)}, f32[4]{0:T(128)}, u32[]{:S(2)}) copy-start(f32[4]{0:T(128)} %param.18) | copy-start | bytes 52
  45.0 19.2 %copy-start.8 = (f32[3]{0:T(128)S(1)}, f32[3]{0:T(128)}, u32[]{:S(2)}) copy-start(f32[3]{0:T(128)} %param.21) | copy-start | bytes 40
  66.8 241.5 %copy-start.9 = (s32[4]{0:T(128)S(1)}, s32[4]{0:T(128)}, u32[]{:S(2)}) copy-start(s32[4]{0:T(128)} %param.15) | copy-start | bytes 52
  73.6 329.2 %all-to-all-start = ((f32[1,4,128,2048]{3,1,0,2:T(4,128)}), f32[1,4,128,2048]{3,1,0,2:T(4,128)}, u32[]{:S(2)}, u32[]{:S(2)}) async-start(f32[1,4,128,2048]{3,1,0,2:T(4,128)} %bitcast.118), calls=%async_computation | async-start | bytes 8388608 | tf_op jit(solution)/shard_map/all_to_all | solution.py:102
  430.0 1.0 copy-start.3
where the time goes:
time: 438 us; the launch traced here: 431 us
  starting transfers between devices  245 us (56%)
  waiting for transfers between devices  95.5 us (22%)
  local copies, waits for them, and re-layouts  71 us (16%)
  other arithmetic  18.4 us (4%)
    all_to_all x1, starting transfers between devices, per_device(): lax.all_to_all(layer_image[None], 'depth', split_axis=2, concat_axis=0, t...  235 us
    all_to_all x1, waiting for transfers between devices, per_device(): lax.all_to_all(layer_image[None], 'depth', split_axis=2, concat_axis=0, t...  94.6 us
    concatenate x2, local copies, waits for them, and re-layouts, with_halo(): x = jnp.concatenate([before, x, after], axis=dim)  30.2 us
    unnamed x11, local copies, waits for them, and re-layouts  17.3 us
  transfers between devices with their start and end apart: 5, of which 2 were waited for; matrix products, arithmetic and copies ran while one was open for 3% of the time, Pallas kernels for 0%

commit v1 on v0

--- a/solution.py
+++ b/solution.py
@@ -5,6 +5,28 @@
 
 slab_depth = 8
 absorption = 0.08
+
+
+def in_blocks(array, dim, size):
+    before, after = (array.shape[:dim], array.shape[dim + 1 :])
+    return jnp.moveaxis(array.reshape(*before, size, -1, *after), dim, 0)
+
+
+def in_order(parts, dim):
+    parts = jnp.moveaxis(parts, 0, dim)
+    shape = parts.shape
+    return parts.reshape(*shape[:dim], shape[dim] * shape[dim + 1], *shape[dim + 2 :])
+
+
+def pairwise_exchange(x, axis, split_dim, concat_dim):
+    peers, index = (lax.axis_size(axis), lax.axis_index(axis))
+    blocks = in_blocks(x, split_dim, peers)
+    outs = [blocks[index]]
+    for turn in range(1, peers):
+        sent = blocks[index ^ turn]
+        outs.append(lax.ppermute(sent, axis, [(i, i ^ turn) for i in range(peers)]))
+    blocks = jnp.stack(outs)[index ^ jnp.arange(peers)]
+    return in_order(blocks, concat_dim)
 
 
 def with_halo(x, sides, width):
@@ -98,9 +120,7 @@
         return march_brick(padded, bump_center, bump_width, bump_height, bump_color, light_dir)
 
     layer_image = lax.cond(empty[0, 0, 0] == 1, blank_layer, lit_layer)
-    band_rows = composite(
-        lax.all_to_all(layer_image[None], "depth", split_axis=2, concat_axis=0, tiled=True), order
-    )
+    band_rows = composite(pairwise_exchange(layer_image[None], "depth", 2, 0), order)
     return band_rows[None]
 
 

time: 438 us -> 413 us (0.943)
  the two profiles are of different devices: /device:TPU:5 before, /device:TPU:20 now
where the time goes in v1:
time: 413 us; the launch traced here: 411 us
  starting transfers between devices  229 us (55%)
  waiting for transfers between devices  92.1 us (22%)
  local copies, waits for them, and re-layouts  66.3 us (16%)
  other arithmetic  22.7 us (5%)
    ppermute x3, starting transfers between devices, pairwise_exchange(): outs.append(lax.ppermute(sent, axis, [(i, i ^ turn) for i in range(peers)]))  219 us
    ppermute x3, waiting for transfers between devices, pairwise_exchange(): outs.append(lax.ppermute(sent, axis, [(i, i ^ turn) for i in range(peers)]))  90.2 us
    concatenate x2, local copies, waits for them, and re-layouts, with_halo(): x = jnp.concatenate([before, x, after], axis=dim)  30.2 us
    unnamed x11, local copies, waits for them, and re-layouts  17.3 us
  transfers between devices with their start and end apart: 7, of which 4 were waited for; matrix products, arithmetic and copies ran while one was open for 3% of the time, Pallas kernels for 0%

profile of v1, /device:TPU:20, one launch (start us, length us, event | category | flops | bytes accessed | tf_op | source)
XLA Modules:
  0.0 410.8 jit_solution(9506762009108148038)
XLA Ops:
  0.0 11.8 %copy.31 = bf16[1,18,128,2048]{3,1,2,0:T(8,128)(2,1)S(1)} copy(bf16[1,18,128,2048]{3,2,1,0:T(8,128)(2,1)} %param.14) | data formatting | bytes 18874368 | tf_op args[0]
  11.8 1.7 collective-permute-start
  14.9 1.9 collective-permute-done.1
  16.7 3.0 pad_maximum_fusion.1
  19.7 4.6 %copy-done.2 = bf16[18,130,2048]{2,0,1:T(8,128)(2,1)} copy-done((bf16[18,130,2048]{2,0,1:T(8,128)(2,1)}, bf16[18,130,2048]{2,0,1:T(8,128)(2,1)S(1)}, u32[]{:S(2)}) %copy-start.2) | copy-done | bytes 9584664
  25.4 3.4 collective-permute-start.2
  29.5 3.3 collective-permute-start.3
  33.5 11.0 %copy.28 = bf16[18,130,2048]{2,1,0:T(8,128)(2,1)} copy(bf16[18,130,2048]{2,0,1:T(8,128)(2,1)} %copy-done.2) | data formatting | bytes 19169280 | tf_op jit(solution)/shard_map/concatenate | solution.py:41
  45.3 19.2 %concatenate.18 = bf16[18,130,2050]{2,1,0:T(8,128)(2,1)} concatenate(bf16[18,130,1]{2,1,0:T(8,128)(2,1)S(1)} %copy.27, bf16[18,130,2048]{2,1,0:T(8,128)(2,1)} %copy.28, bf16[18,130,1]{2,1,0:T(8,128)(2,1)S(1)} %copy.29), dimensions={2} | concatenate | bytes 19188000 | tf_op jit(solution)/shard_map/concatenate | solution.py:41
  64.5 2.5 conditional.1
  64.5 2.5 reshape_broadcast_in_dim.4
  67.0 3.9 dynamic-slice_bitcast_fusion.3
  70.9 217.5 %collective-permute-start.4 = (f32[1,4,32,2048]{3,2,1,0:T(8,128)}, f32[1,4,32,2048]{3,2,1,0:T(8,128)}, u32[]{:S(2)}, u32[]{:S(2)}) collective-permute-start(f32[1,4,32,2048]{3,2,1,0:T(8,128)} %get-tuple-element.365), channel_id=1, source_target_pairs={{0,8},{8,0},{16,24},{24,16},{1,9},{9,1},{17,25},{25,17},{2,10},{10... | collective-permute-start | bytes 3145736 | tf_op jit(solution)/shard_map/ppermute | solution.py:27
  289.9 40.2 %collective-permute-done.4 = f32[1,4,32,2048]{3,2,1,0:T(8,128)} collective-permute-done((f32[1,4,32,2048]{3,2,1,0:T(8,128)}, f32[1,4,32,2048]{3,2,1,0:T(8,128)}, u32[]{:S(2)}, u32[]{:S(2)}) %collective-permute-start.4) | collective-permute-done | bytes 1048608 | tf_op jit(solution)/shard_map/ppermute | solution.py:27
  330.1 27.5 %collective-permute-done.5 = f32[1,4,32,2048]{3,2,1,0:T(8,128)} collective-permute-done((f32[1,4,32,2048]{3,2,1,0:T(8,128)}, f32[1,4,32,2048]{3,2,1,0:T(8,128)}, u32[]{:S(2)}, u32[]{:S(2)}) %collective-permute-start.5) | collective-permute-done | bytes 1048608 | tf_op jit(solution)/shard_map/ppermute | solution.py:27
  357.6 22.5 %collective-permute-done.6 = f32[1,4,32,2048]{3,2,1,0:T(8,128)} collective-permute-done((f32[1,4,32,2048]{3,2,1,0:T(8,128)S(1)}, f32[1,4,32,2048]{3,2,1,0:T(8,128)}, u32[]{:S(2)}, u32[]{:S(2)}) %collective-permute-start.6) | collective-permute-done | bytes 1048608 | tf_op jit(solution)/shard_map/ppermute | solution.py:27
  380.1 4.2 %maximum_bitcast_fusion = f32[4,4,32,2048]{3,2,1,0:T(8,128)} fusion(f32[1,1,4,32,2048]{4,3,2,1,0:T(8,128)} %bitcast.17, f32[1,1,4,32,2048]{4,3,2,1,0:T(8,128)} %bitcast.15, f32[1,1,4,32,2048]{4,3,2,1,0:T(8,128)} %bitcast.13, f32[1,1,4,32,2048]{4,3,2,1,0:T(8,128)S(1)} %get-tuple-element.362), kind=kLoop, calls=%fused_computation.38 | loop fusion | flops 3145728 | bytes 8388608 | tf_op jit(solution)/shard_map/stack | solution.py:28
  384.4 5.0 %gather_fusion = f32[4,4,32,2048]{3,2,1,0:T(8,128)} fusion(f32[4,4,32,2048]{3,2,1,0:T(8,128)} %maximum_bitcast_fusion, s32[1024]{0:T(1024)S(1)} %pad_clamp_fusion.1), kind=kCustom, calls=%fused_computation | custom fusion | bytes 8388624 | tf_op jit(solution)/shard_map/gather | solution.py:28
  389.3 5.0 %gather_fusion.1 = f32[4,4,32,2048]{3,2,1,0:T(8,128)} fusion(f32[4,4,32,2048]{3,2,1,0:T(8,128)} %gather_fusion, s32[1024]{0:T(1024)S(1)} %pad_clamp_fusion), kind=kCustom, calls=%fused_computation.1 | custom fusion | bytes 8388624 | tf_op jit(solution)/shard_map/jit(_take)/gather | solution.py:96
  394.3 4.9 %broadcast_select_fusion.2 = f32[4,4,32,2048]{3,2,1,0:T(8,128)} fusion(f32[4,4,32,2048]{3,2,1,0:T(8,128)} %gather_fusion.1, pred[4]{0:T(512)(128)(4,1)S(1)} %compare_and_fusion), kind=kLoop, calls=%fused_computation.39 | loop fusion | flops 1048576 | bytes 8388612 | tf_op jit(solution)/shard_map/jit(_take)/select_n | solution.py:96
  399.2 10.6 %while.28 = (s32[]{:T(128)}, f32[32,2048]{1,0:T(8,128)S(1)}, f32[4,32,2048]{2,1,0:T(8,128)S(1)}, f32[4,4,32,2048]{3,2,1,0:T(8,128)}, s32[]{:T(128)}, /*index=5*/s32[]{:T(128)}, s32[]{}) while((s32[]{:T(128)}, f32[32,2048]{1,0:T(8,128)S(1)}, f32[4,32,2048]{2,1,0:T(8,128)S(1)}, f32[4,4,32,2048]{3,2,1,0:T(8,128)}, s32[]{:T(128)}, ...), condition=%wide.region_9.10_spmd.clone, body=%wide.region_8.9_spmd.clone.sunk | while | flops 983044 | bytes 4456560 | solution.py:107
  400.2 1.6 fusion.28
  402.9 1.6 fusion.28
  405.5 1.6 fusion.28
  (33 shorter events, 12.1 us)
Async XLA Ops:
  11.8 3.1 collective-permute-start
  13.5 3.2 collective-permute-start.1
  19.7 4.6 %copy-start.2 = (bf16[18,130,2048]{2,0,1:T(8,128)(2,1)}, bf16[18,130,2048]{2,0,1:T(8,128)(2,1)S(1)}, u32[]{:S(2)}) copy-start(bf16[18,130,2048]{2,0,1:T(8,128)(2,1)S(1)} %pad_maximum_fusion.1) | copy-start | bytes 28753924
  25.4 19.1 %collective-permute-start.2 = (bf16[18,130,1]{1,0,2:T(8,128)(2,1)S(1)}, bf16[18,130,1]{1,0,2:T(8,128)(2,1)S(1)}, u32[]{:S(2)}, u32[]{:S(2)}) collective-permute-start(bf16[18,130,1]{1,0,2:T(8,128)(2,1)S(1)} %copy.25), channel_id=1, source_target_pairs={{0,1},{1,2},{2,3},{4,5},{5,6},{6,7},{8,9},{9,10},{10,11},{12,13},{... | collective-permute-start | bytes 14048 | tf_op jit(solution)/shard_map/ppermute | solution.py:39
  29.5 15.4 %collective-permute-start.3 = (bf16[18,130,1]{1,0,2:T(8,128)(2,1)S(1)}, bf16[18,130,1]{1,0,2:T(8,128)(2,1)S(1)}, u32[]{:S(2)}, u32[]{:S(2)}) collective-permute-start(bf16[18,130,1]{1,0,2:T(8,128)(2,1)S(1)} %copy.26), channel_id=1, source_target_pairs={{1,0},{2,1},{3,2},{5,4},{6,5},{7,6},{9,8},{10,9},{11,10},{13,12},{... | collective-permute-start | bytes 14048 | tf_op jit(solution)/shard_map/ppermute | solution.py:40
  45.3 19.2 %copy-start.7 = (f32[4]{0:T(128)S(1)}, f32[4]{0:T(128)}, u32[]{:S(2)}) copy-start(f32[4]{0:T(128)} %param.18) | copy-start | bytes 52
  45.3 19.2 %copy-start.8 = (f32[3]{0:T(128)S(1)}, f32[3]{0:T(128)}, u32[]{:S(2)}) copy-start(f32[3]{0:T(128)} %param.21) | copy-start | bytes 40
  67.0 222.9 %copy-start.9 = (s32[4]{0:T(128)S(1)}, s32[4]{0:T(128)}, u32[]{:S(2)}) copy-start(s32[4]{0:T(128)} %param.15) | copy-start | bytes 52
  70.9 259.2 %collective-permute-start.4 = (f32[1,4,32,2048]{3,2,1,0:T(8,128)}, f32[1,4,32,2048]{3,2,1,0:T(8,128)}, u32[]{:S(2)}, u32[]{:S(2)}) collective-permute-start(f32[1,4,32,2048]{3,2,1,0:T(8,128)} %get-tuple-element.365), channel_id=1, source_target_pairs={{0,8},{8,0},{16,24},{24,16},{1,9},{9,1},{17,25},{25,17},{2,10},{10... | collective-permute-start | bytes 3145736 | tf_op jit(solution)/shard_map/ppermute | solution.py:27
  288.4 69.2 %collective-permute-start.5 = (f32[1,4,32,2048]{3,2,1,0:T(8,128)}, f32[1,4,32,2048]{3,2,1,0:T(8,128)}, u32[]{:S(2)}, u32[]{:S(2)}) collective-permute-start(f32[1,4,32,2048]{3,2,1,0:T(8,128)} %get-tuple-element.364), channel_id=1, source_target_pairs={{0,16},{8,24},{16,0},{24,8},{1,17},{9,25},{17,1},{25,9},{2,18},{10... | collective-permute-start | bytes 3145736 | tf_op jit(solution)/shard_map/ppermute | solution.py:27
  288.7 91.4 %collective-permute-start.6 = (f32[1,4,32,2048]{3,2,1,0:T(8,128)S(1)}, f32[1,4,32,2048]{3,2,1,0:T(8,128)}, u32[]{:S(2)}, u32[]{:S(2)}) collective-permute-start(f32[1,4,32,2048]{3,2,1,0:T(8,128)S(1)} %get-tuple-element.363), channel_id=1, source_target_pairs={{0,24},{8,16},{16,8},{24,0},{1,25},{9,17},{17,9},{25,1},{2,26},{10... | collective-permute-start | bytes 3145736 | tf_op jit(solution)/shard_map/ppermute | solution.py:27
  409.8 1.0 copy-start.3
